TPU v7x, 32 devices: a whole 2x2x4 slice. The times are simulated.
32 devices in a mesh: row: 8 (over z, x), col: 4 (over y, core).
Axes of the slice: x: 2, y: 2, z: 4, core: 2. Of those that a mesh axis runs over, the one named last changes fastest.
Arguments:
- vectors: float32 [8192, 1024], P(('row', 'col')), may hold values from -6 to 6
- rotation: float32 [1024, 1024], P(None, 'col'), may hold values from -0.1875 to 0.1875
- blocks: bfloat16 [64, 16, 128, 128], P('row'), may hold values from -0.0625 to 0.0625
- cols: int32 [64, 16], P('row'), may hold values from 0 to 15, as said below
- lists: int32 [8, 2, 4], P('row'), may hold values from 0 to 7, as said below
- counts: int32 [8], P('row'), may hold values from 4 to 8, as said below
Outputs:
- filtered: float32 [1024, 8192], P('col', 'row')
Inputs may be any that keep to these rules, and one draw needn't show every extreme that they name: `counts`: at least one group uses all 8 slots. Every entry of lists[r] is below counts[r], and lists[r, j, 0] = counts[r] - 1; entries may repeat. cols[t, 0] = 4 + t % 8, the block row itself; on valid block rows of group r every slot between 4 and 15 that names an own block row is below 4 + counts[r].
All inputs are finite; a program needn't handle non-finite values.
Results may differ from a plain program's by a relative error of at most 0.0065.
Values may be sent and summed in bfloat16 or wider, within the bound.
No kernel may reach another device: no remote copies, remote signals or barrier semaphores. Data moves between devices by JAX's collectives and lax.ppermute only.
A program may use at most 64 MiB of HBM per device.

v0:
```python
import jax
import jax.numpy as jnp
from jax import lax
from jax.sharding import PartitionSpec as P

STEPS = 10


def passed_along(x, axis, by):
    length = lax.axis_size(axis)
    pairs = [(i, i + by) for i in range(length) if 0 <= i + by < length]
    return lax.ppermute(x, axis, pairs)


def apply_blocks(field, blocks, cols, lists, valid):
    lowered = field.astype(jnp.bfloat16)
    up_rows = lowered[:, lists[0, 0], :]
    down_rows = lowered[:, lists[0, 1], :]
    from_prev = passed_along(up_rows, "row", 1)
    from_next = passed_along(down_rows, "row", -1)
    source = jnp.concatenate([from_prev, lowered, from_next], axis=1)
    picked = source[:, cols, :]
    result = jnp.einsum("cbkj,bkij->cbi", picked, blocks, preferred_element_type=jnp.float32)
    return result * valid[None, :, None]


def body(vectors, rotation, blocks, cols, lists, counts):
    cap = blocks.shape[0]
    width = blocks.shape[2]
    panel = lax.dot_general(
        rotation,
        lax.all_gather(vectors, "col", axis=0, tiled=True),
        (((0,), (1,)), ((), ())),
        precision=lax.Precision.HIGHEST,
        preferred_element_type=jnp.float32,
    )
    panel_cols = panel.shape[0]
    valid = (jnp.arange(cap, dtype=jnp.int32) < counts[0]).astype(jnp.float32)
    previous = panel.reshape(panel_cols, cap, width) * valid[None, :, None]
    current = apply_blocks(previous, blocks, cols, lists, valid)

    def advance(index, carry):
        older, newer = carry
        return (newer, 2.0 * apply_blocks(newer, blocks, cols, lists, valid) - older)

    previous, current = lax.fori_loop(0, STEPS - 1, advance, (previous, current))
    return current.reshape(panel_cols, cap * width)


def solution(mesh):
    return jax.shard_map(
        body,
        mesh=mesh,
        in_specs=(
            P(("row", "col"), None),
            P(None, "col"),
            P("row", None, None, None),
            P("row", None),
            P("row", None, None),
            P("row"),
        ),
        out_specs=P("col", "row"),
        check_vma=False,
    )
```

profile of v0, /device:TPU:0, one launch (start us, length us, event | category | flops | bytes accessed | tf_op | source)
XLA Modules:
  0.0 394.8 jit_solution(11017136291069954017)
XLA Ops:
  8.7 37.4 %all-gather.2.cloned.1.call-done = f32[1024,1024]{1,0:T(8,128)} async-done(((f32[256,1024]{1,0:T(8,128)}), f32[1024,1024]{1,0:T(8,128)}) %all-gather.2.cloned.1.call-update) | async-done | bytes 4194320 | tf_op jit(solution)/shard_map/all_gather | solution.py:32
  46.1 8.7 %convolution_bitcast_fusion.2 = f32[32,8,8,128]{3,2,1,0:T(8,128)S(1)} fusion(f32[1024,256]{1,0:T(8,128)S(1)} %copy-done, f32[1024,1024]{1,0:T(8,128)} %all-gather.2.cloned.1.call-done), kind=kOutput, calls=%fused_computation.25 | convolution fusion | flops 3221225472 | bytes 6291456 | tf_op jit(solution)/shard_map/dot_general | solution.py:30
  62.1 9.5 %collective-permute-done.2 = bf16[256,4,128]{2,0,1:T(8,128)(2,1)S(1)} collective-permute-done((bf16[256,4,128]{2,0,1:T(8,128)(2,1)S(1)}, bf16[256,4,128]{2,0,1:T(8,128)(2,1)S(1)}, u32[]{:S(2)}, u32[]{:S(2)}) %collective-permute-start.2) | collective-permute-done | bytes 262176 | tf_op jit(solution)/shard_map/ppermute | solution.py:12
  71.7 6.6 %gather_fusion.5 = bf16[128,256,128]{2,1,0:T(8,128)(2,1)} fusion(bf16[256,16,128]{2,0,1:T(8,128)(2,1)S(1)} %pad_maximum_fusion.1, s32[1024]{0:T(1024)S(1)} %pad_clamp_fusion.3), kind=kCustom, calls=%fused_computation.5 | custom fusion | bytes 16777728 | tf_op jit(solution)/shard_map/gather | solution.py:22
  78.3 6.9 %fusion.9 = f32[256,8,128]{2,0,1:T(8,128)S(1)} fusion(bf16[256,8,16,128]{3,0,2,1:T(8,128)(2,1)} %bitcast.93, bf16[8,16,128,128]{3,2,1,0:T(8,128)(2,1)} %param.10, f32[8]{0:T(128)S(1)} %compare_convert_fusion.1), kind=kOutput, calls=%fused_computation.24 | convolution fusion | flops 1074003968 | bytes 13631520 | tf_op jit(solution)/shard_map/cbkj,bkij->cbi/dot_general | solution.py:23
  85.2 301.6 %while.13 = (s32[]{:T(128)}, f32[256,8,128]{2,0,1:T(8,128)}, f32[256,8,128]{2,0,1:T(8,128)S(1)}, s32[1,2,4]{2,1,0:T(2,128)S(1)}, s32[8,16]{1,0:T(8,128)S(1)}, /*...) while((s32[]{:T(128)}, f32[256,8,128]{2,0,1:T(8,128)}, f32[256,8,128]{2,0,1:T(8,128)S(1)}, ...), condition=%wide.region_1.0_spmd.clone, body=%wide.region_0.0_spmd.clone.sunk | while | flops 1075842432 | bytes 44580228 | solution.py:46
  103.6 6.6 %gather_fusion.2 = bf16[128,256,128]{2,1,0:T(8,128)(2,1)} fusion(bf16[256,16,128]{2,0,1:T(8,128)(2,1)S(1)} %pad_maximum_fusion.3, s32[1024]{0:T(1024)S(1)} %pad_clamp_fusion.9), kind=kCustom, calls=%fused_computation.2.clone.clone.1 | custom fusion | bytes 16777728 | tf_op jit(solution)/shard_map/while/body/eval_jaxpr/gather | solution.py:22
  110.2 7.2 %fusion.27 = f32[256,8,128]{2,0,1:T(8,128)S(1)} fusion(f32[256,8,128]{2,0,1:T(8,128)} %get-tuple-element.144, bf16[256,8,16,128]{3,0,2,1:T(8,128)(2,1)} %bitcast.92, bf16[8,16,128,128]{3,2,1,0:T(8,128)(2,1)} %get-tuple-element.156, f32[8]{0:T(128)S(1)} %compare_convert_fusion.3), kind=kOutput, calls=%fused_computation.11.clone.1 | convolution fusion | flops 1074528256 | bytes 14680096 | tf_op jit(solution)/shard_map/while/body/eval_jaxpr/cbkj,bkij->cbi/dot_general | solution.py:23
  137.1 6.6 %gather_fusion.2 = bf16[128,256,128]{2,1,0:T(8,128)(2,1)} fusion(bf16[256,16,128]{2,0,1:T(8,128)(2,1)S(1)} %pad_maximum_fusion.3, s32[1024]{0:T(1024)S(1)} %pad_clamp_fusion.9), kind=kCustom, calls=%fused_computation.2.clone.clone.1 | custom fusion | bytes 16777728 | tf_op jit(solution)/shard_map/while/body/eval_jaxpr/gather | solution.py:22
  143.7 7.2 %fusion.27 = f32[256,8,128]{2,0,1:T(8,128)S(1)} fusion(f32[256,8,128]{2,0,1:T(8,128)} %get-tuple-element.144, bf16[256,8,16,128]{3,0,2,1:T(8,128)(2,1)} %bitcast.92, bf16[8,16,128,128]{3,2,1,0:T(8,128)(2,1)} %get-tuple-element.156, f32[8]{0:T(128)S(1)} %compare_convert_fusion.3), kind=kOutput, calls=%fused_computation.11.clone.1 | convolution fusion | flops 1074528256 | bytes 14680096 | tf_op jit(solution)/shard_map/while/body/eval_jaxpr/cbkj,bkij->cbi/dot_general | solution.py:23
  170.7 6.6 %gather_fusion.2 = bf16[128,256,128]{2,1,0:T(8,128)(2,1)} fusion(bf16[256,16,128]{2,0,1:T(8,128)(2,1)S(1)} %pad_maximum_fusion.3, s32[1024]{0:T(1024)S(1)} %pad_clamp_fusion.9), kind=kCustom, calls=%fused_computation.2.clone.clone.1 | custom fusion | bytes 16777728 | tf_op jit(solution)/shard_map/while/body/eval_jaxpr/gather | solution.py:22
  177.2 7.2 %fusion.27 = f32[256,8,128]{2,0,1:T(8,128)S(1)} fusion(f32[256,8,128]{2,0,1:T(8,128)} %get-tuple-element.144, bf16[256,8,16,128]{3,0,2,1:T(8,128)(2,1)} %bitcast.92, bf16[8,16,128,128]{3,2,1,0:T(8,128)(2,1)} %get-tuple-element.156, f32[8]{0:T(128)S(1)} %compare_convert_fusion.3), kind=kOutput, calls=%fused_computation.11.clone.1 | convolution fusion | flops 1074528256 | bytes 14680096 | tf_op jit(solution)/shard_map/while/body/eval_jaxpr/cbkj,bkij->cbi/dot_general | solution.py:23
  204.2 6.6 %gather_fusion.2 = bf16[128,256,128]{2,1,0:T(8,128)(2,1)} fusion(bf16[256,16,128]{2,0,1:T(8,128)(2,1)S(1)} %pad_maximum_fusion.3, s32[1024]{0:T(1024)S(1)} %pad_clamp_fusion.9), kind=kCustom, calls=%fused_computation.2.clone.clone.1 | custom fusion | bytes 16777728 | tf_op jit(solution)/shard_map/while/body/eval_jaxpr/gather | solution.py:22
  210.8 7.2 %fusion.27 = f32[256,8,128]{2,0,1:T(8,128)S(1)} fusion(f32[256,8,128]{2,0,1:T(8,128)} %get-tuple-element.144, bf16[256,8,16,128]{3,0,2,1:T(8,128)(2,1)} %bitcast.92, bf16[8,16,128,128]{3,2,1,0:T(8,128)(2,1)} %get-tuple-element.156, f32[8]{0:T(128)S(1)} %compare_convert_fusion.3), kind=kOutput, calls=%fused_computation.11.clone.1 | convolution fusion | flops 1074528256 | bytes 14680096 | tf_op jit(solution)/shard_map/while/body/eval_jaxpr/cbkj,bkij->cbi/dot_general | solution.py:23
  237.8 6.6 %gather_fusion.2 = bf16[128,256,128]{2,1,0:T(8,128)(2,1)} fusion(bf16[256,16,128]{2,0,1:T(8,128)(2,1)S(1)} %pad_maximum_fusion.3, s32[1024]{0:T(1024)S(1)} %pad_clamp_fusion.9), kind=kCustom, calls=%fused_computation.2.clone.clone.1 | custom fusion | bytes 16777728 | tf_op jit(solution)/shard_map/while/body/eval_jaxpr/gather | solution.py:22
  244.3 7.2 %fusion.27 = f32[256,8,128]{2,0,1:T(8,128)S(1)} fusion(f32[256,8,128]{2,0,1:T(8,128)} %get-tuple-element.144, bf16[256,8,16,128]{3,0,2,1:T(8,128)(2,1)} %bitcast.92, bf16[8,16,128,128]{3,2,1,0:T(8,128)(2,1)} %get-tuple-element.156, f32[8]{0:T(128)S(1)} %compare_convert_fusion.3), kind=kOutput, calls=%fused_computation.11.clone.1 | convolution fusion | flops 1074528256 | bytes 14680096 | tf_op jit(solution)/shard_map/while/body/eval_jaxpr/cbkj,bkij->cbi/dot_general | solution.py:23
  271.3 6.6 %gather_fusion.2 = bf16[128,256,128]{2,1,0:T(8,128)(2,1)} fusion(bf16[256,16,128]{2,0,1:T(8,128)(2,1)S(1)} %pad_maximum_fusion.3, s32[1024]{0:T(1024)S(1)} %pad_clamp_fusion.9), kind=kCustom, calls=%fused_computation.2.clone.clone.1 | custom fusion | bytes 16777728 | tf_op jit(solution)/shard_map/while/body/eval_jaxpr/gather | solution.py:22
  277.9 7.2 %fusion.27 = f32[256,8,128]{2,0,1:T(8,128)S(1)} fusion(f32[256,8,128]{2,0,1:T(8,128)} %get-tuple-element.144, bf16[256,8,16,128]{3,0,2,1:T(8,128)(2,1)} %bitcast.92, bf16[8,16,128,128]{3,2,1,0:T(8,128)(2,1)} %get-tuple-element.156, f32[8]{0:T(128)S(1)} %compare_convert_fusion.3), kind=kOutput, calls=%fused_computation.11.clone.1 | convolution fusion | flops 1074528256 | bytes 14680096 | tf_op jit(solution)/shard_map/while/body/eval_jaxpr/cbkj,bkij->cbi/dot_general | solution.py:23
  304.9 6.6 %gather_fusion.2 = bf16[128,256,128]{2,1,0:T(8,128)(2,1)} fusion(bf16[256,16,128]{2,0,1:T(8,128)(2,1)S(1)} %pad_maximum_fusion.3, s32[1024]{0:T(1024)S(1)} %pad_clamp_fusion.9), kind=kCustom, calls=%fused_computation.2.clone.clone.1 | custom fusion | bytes 16777728 | tf_op jit(solution)/shard_map/while/body/eval_jaxpr/gather | solution.py:22
  311.5 7.2 %fusion.27 = f32[256,8,128]{2,0,1:T(8,128)S(1)} fusion(f32[256,8,128]{2,0,1:T(8,128)} %get-tuple-element.144, bf16[256,8,16,128]{3,0,2,1:T(8,128)(2,1)} %bitcast.92, bf16[8,16,128,128]{3,2,1,0:T(8,128)(2,1)} %get-tuple-element.156, f32[8]{0:T(128)S(1)} %compare_convert_fusion.3), kind=kOutput, calls=%fused_computation.11.clone.1 | convolution fusion | flops 1074528256 | bytes 14680096 | tf_op jit(solution)/shard_map/while/body/eval_jaxpr/cbkj,bkij->cbi/dot_general | solution.py:23
  338.4 6.6 %gather_fusion.2 = bf16[128,256,128]{2,1,0:T(8,128)(2,1)} fusion(bf16[256,16,128]{2,0,1:T(8,128)(2,1)S(1)} %pad_maximum_fusion.3, s32[1024]{0:T(1024)S(1)} %pad_clamp_fusion.9), kind=kCustom, calls=%fused_computation.2.clone.clone.1 | custom fusion | bytes 16777728 | tf_op jit(solution)/shard_map/while/body/eval_jaxpr/gather | solution.py:22
  345.0 7.2 %fusion.27 = f32[256,8,128]{2,0,1:T(8,128)S(1)} fusion(f32[256,8,128]{2,0,1:T(8,128)} %get-tuple-element.144, bf16[256,8,16,128]{3,0,2,1:T(8,128)(2,1)} %bitcast.92, bf16[8,16,128,128]{3,2,1,0:T(8,128)(2,1)} %get-tuple-element.156, f32[8]{0:T(128)S(1)} %compare_convert_fusion.3), kind=kOutput, calls=%fused_computation.11.clone.1 | convolution fusion | flops 1074528256 | bytes 14680096 | tf_op jit(solution)/shard_map/while/body/eval_jaxpr/cbkj,bkij->cbi/dot_general | solution.py:23
  372.0 6.6 %gather_fusion.2 = bf16[128,256,128]{2,1,0:T(8,128)(2,1)} fusion(bf16[256,16,128]{2,0,1:T(8,128)(2,1)S(1)} %pad_maximum_fusion.3, s32[1024]{0:T(1024)S(1)} %pad_clamp_fusion.9), kind=kCustom, calls=%fused_computation.2.clone.clone.1 | custom fusion | bytes 16777728 | tf_op jit(solution)/shard_map/while/body/eval_jaxpr/gather | solution.py:22
  378.6 7.2 %fusion.27 = f32[256,8,128]{2,0,1:T(8,128)S(1)} fusion(f32[256,8,128]{2,0,1:T(8,128)} %get-tuple-element.144, bf16[256,8,16,128]{3,0,2,1:T(8,128)(2,1)} %bitcast.92, bf16[8,16,128,128]{3,2,1,0:T(8,128)(2,1)} %get-tuple-element.156, f32[8]{0:T(128)S(1)} %compare_convert_fusion.3), kind=kOutput, calls=%fused_computation.11.clone.1 | convolution fusion | flops 1074528256 | bytes 14680096 | tf_op jit(solution)/shard_map/while/body/eval_jaxpr/cbkj,bkij->cbi/dot_general | solution.py:23
  (184 shorter events, 186.6 us)
Async XLA Ops:
  6.5 39.6 %copy-start = (f32[1024,256]{1,0:T(8,128)S(1)}, f32[1024,256]{1,0:T(8,128)}, u32[]{:S(2)}) copy-start(f32[1024,256]{1,0:T(8,128)} %param.9) | copy-start | bytes 3145732
  6.5 55.4 %copy-start.2 = (s32[8,16]{1,0:T(8,128)S(1)}, s32[8,16]{1,0:T(8,128)}, u32[]{:S(2)}) copy-start(s32[8,16]{1,0:T(8,128)} %param.11) | copy-start | bytes 1540
  6.5 39.6 %all-gather.2.cloned.1.call-start = ((), (), s32[]{:S(2)}) async-start(), calls=%async_computation | async-start | bytes 5242880 | tf_op jit(solution)/shard_map/all_gather | solution.py:32
  56.7 14.9 %collective-permute-start.2 = (bf16[256,4,128]{2,0,1:T(8,128)(2,1)S(1)}, bf16[256,4,128]{2,0,1:T(8,128)(2,1)S(1)}, u32[]{:S(2)}, u32[]{:S(2)}) collective-permute-start(bf16[256,4,128]{2,0,1:T(8,128)(2,1)S(1)} %bitcast.96), channel_id=1, source_target_pairs={{0,4},{4,8},{8,12},{12,16},{16,20},{20,24},{24,28},{1,5},{5,9},{9,... | collective-permute-start | bytes 786440 | tf_op jit(solution)/shard_map/ppermute | solution.py:12
  60.7 10.9 %collective-permute-start.3 = (bf16[256,4,128]{2,0,1:T(8,128)(2,1)S(1)}, bf16[256,4,128]{2,0,1:T(8,128)(2,1)S(1)}, u32[]{:S(2)}, u32[]{:S(2)}) collective-permute-start(bf16[256,4,128]{2,0,1:T(8,128)(2,1)S(1)} %bitcast.97), channel_id=1, source_target_pairs={{4,0},{8,4},{12,8},{16,12},{20,16},{24,20},{28,24},{5,1},{9,5},{13... | collective-permute-start | bytes 786440 | tf_op jit(solution)/shard_map/ppermute | solution.py:12
  86.0 10.2 %collective-permute-start = (bf16[256,4,128]{2,0,1:T(8,128)(2,1)S(1)}, bf16[256,4,128]{2,0,1:T(8,128)(2,1)S(1)}, u32[]{:S(2)}, u32[]{:S(2)}) collective-permute-start(bf16[256,4,128]{2,0,1:T(8,128)(2,1)S(1)} %bitcast.94), channel_id=1, source_target_pairs={{4,0},{8,4},{12,8},{16,12},{20,16},{24,20},{28,24},{5,1},{9,5},{13... | collective-permute-start | bytes 786440 | tf_op jit(solution)/shard_map/while/body/eval_jaxpr/ppermute | solution.py:12
  87.9 14.5 %collective-permute-start.1 = (bf16[256,4,128]{2,0,1:T(8,128)(2,1)S(1)}, bf16[256,4,128]{2,0,1:T(8,128)(2,1)}, u32[]{:S(2)}, u32[]{:S(2)}) collective-permute-start(bf16[256,4,128]{2,0,1:T(8,128)(2,1)S(1)} %bitcast.95), channel_id=1, source_target_pairs={{0,4},{4,8},{8,12},{12,16},{16,20},{20,24},{24,28},{1,5},{5,9},{9,... | collective-permute-start | bytes 786440 | tf_op jit(solution)/shard_map/while/body/eval_jaxpr/ppermute | solution.py:12
  119.1 11.0 %collective-permute-start = (bf16[256,4,128]{2,0,1:T(8,128)(2,1)S(1)}, bf16[256,4,128]{2,0,1:T(8,128)(2,1)S(1)}, u32[]{:S(2)}, u32[]{:S(2)}) collective-permute-start(bf16[256,4,128]{2,0,1:T(8,128)(2,1)S(1)} %bitcast.94), channel_id=1, source_target_pairs={{4,0},{8,4},{12,8},{16,12},{20,16},{24,20},{28,24},{5,1},{9,5},{13... | collective-permute-start | bytes 786440 | tf_op jit(solution)/shard_map/while/body/eval_jaxpr/ppermute | solution.py:12
  121.1 14.8 %collective-permute-start.1 = (bf16[256,4,128]{2,0,1:T(8,128)(2,1)S(1)}, bf16[256,4,128]{2,0,1:T(8,128)(2,1)}, u32[]{:S(2)}, u32[]{:S(2)}) collective-permute-start(bf16[256,4,128]{2,0,1:T(8,128)(2,1)S(1)} %bitcast.95), channel_id=1, source_target_pairs={{0,4},{4,8},{8,12},{12,16},{16,20},{20,24},{24,28},{1,5},{5,9},{9,... | collective-permute-start | bytes 786440 | tf_op jit(solution)/shard_map/while/body/eval_jaxpr/ppermute | solution.py:12
  152.7 11.0 %collective-permute-start = (bf16[256,4,128]{2,0,1:T(8,128)(2,1)S(1)}, bf16[256,4,128]{2,0,1:T(8,128)(2,1)S(1)}, u32[]{:S(2)}, u32[]{:S(2)}) collective-permute-start(bf16[256,4,128]{2,0,1:T(8,128)(2,1)S(1)} %bitcast.94), channel_id=1, source_target_pairs={{4,0},{8,4},{12,8},{16,12},{20,16},{24,20},{28,24},{5,1},{9,5},{13... | collective-permute-start | bytes 786440 | tf_op jit(solution)/shard_map/while/body/eval_jaxpr/ppermute | solution.py:12
  154.6 14.8 %collective-permute-start.1 = (bf16[256,4,128]{2,0,1:T(8,128)(2,1)S(1)}, bf16[256,4,128]{2,0,1:T(8,128)(2,1)}, u32[]{:S(2)}, u32[]{:S(2)}) collective-permute-start(bf16[256,4,128]{2,0,1:T(8,128)(2,1)S(1)} %bitcast.95), channel_id=1, source_target_pairs={{0,4},{4,8},{8,12},{12,16},{16,20},{20,24},{24,28},{1,5},{5,9},{9,... | collective-permute-start | bytes 786440 | tf_op jit(solution)/shard_map/while/body/eval_jaxpr/ppermute | solution.py:12
  186.2 11.0 %collective-permute-start = (bf16[256,4,128]{2,0,1:T(8,128)(2,1)S(1)}, bf16[256,4,128]{2,0,1:T(8,128)(2,1)S(1)}, u32[]{:S(2)}, u32[]{:S(2)}) collective-permute-start(bf16[256,4,128]{2,0,1:T(8,128)(2,1)S(1)} %bitcast.94), channel_id=1, source_target_pairs={{4,0},{8,4},{12,8},{16,12},{20,16},{24,20},{28,24},{5,1},{9,5},{13... | collective-permute-start | bytes 786440 | tf_op jit(solution)/shard_map/while/body/eval_jaxpr/ppermute | solution.py:12
  188.2 14.8 %collective-permute-start.1 = (bf16[256,4,128]{2,0,1:T(8,128)(2,1)S(1)}, bf16[256,4,128]{2,0,1:T(8,128)(2,1)}, u32[]{:S(2)}, u32[]{:S(2)}) collective-permute-start(bf16[256,4,128]{2,0,1:T(8,128)(2,1)S(1)} %bitcast.95), channel_id=1, source_target_pairs={{0,4},{4,8},{8,12},{12,16},{16,20},{20,24},{24,28},{1,5},{5,9},{9,... | collective-permute-start | bytes 786440 | tf_op jit(solution)/shard_map/while/body/eval_jaxpr/ppermute | solution.py:12
  219.8 11.0 %collective-permute-start = (bf16[256,4,128]{2,0,1:T(8,128)(2,1)S(1)}, bf16[256,4,128]{2,0,1:T(8,128)(2,1)S(1)}, u32[]{:S(2)}, u32[]{:S(2)}) collective-permute-start(bf16[256,4,128]{2,0,1:T(8,128)(2,1)S(1)} %bitcast.94), channel_id=1, source_target_pairs={{4,0},{8,4},{12,8},{16,12},{20,16},{24,20},{28,24},{5,1},{9,5},{13... | collective-permute-start | bytes 786440 | tf_op jit(solution)/shard_map/while/body/eval_jaxpr/ppermute | solution.py:12
  221.7 14.8 %collective-permute-start.1 = (bf16[256,4,128]{2,0,1:T(8,128)(2,1)S(1)}, bf16[256,4,128]{2,0,1:T(8,128)(2,1)}, u32[]{:S(2)}, u32[]{:S(2)}) collective-permute-start(bf16[256,4,128]{2,0,1:T(8,128)(2,1)S(1)} %bitcast.95), channel_id=1, source_target_pairs={{0,4},{4,8},{8,12},{12,16},{16,20},{20,24},{24,28},{1,5},{5,9},{9,... | collective-permute-start | bytes 786440 | tf_op jit(solution)/shard_map/while/body/eval_jaxpr/ppermute | solution.py:12
  253.3 11.0 %collective-permute-start = (bf16[256,4,128]{2,0,1:T(8,128)(2,1)S(1)}, bf16[256,4,128]{2,0,1:T(8,128)(2,1)S(1)}, u32[]{:S(2)}, u32[]{:S(2)}) collective-permute-start(bf16[256,4,128]{2,0,1:T(8,128)(2,1)S(1)} %bitcast.94), channel_id=1, source_target_pairs={{4,0},{8,4},{12,8},{16,12},{20,16},{24,20},{28,24},{5,1},{9,5},{13... | collective-permute-start | bytes 786440 | tf_op jit(solution)/shard_map/while/body/eval_jaxpr/ppermute | solution.py:12
  255.3 14.8 %collective-permute-start.1 = (bf16[256,4,128]{2,0,1:T(8,128)(2,1)S(1)}, bf16[256,4,128]{2,0,1:T(8,128)(2,1)}, u32[]{:S(2)}, u32[]{:S(2)}) collective-permute-start(bf16[256,4,128]{2,0,1:T(8,128)(2,1)S(1)} %bitcast.95), channel_id=1, source_target_pairs={{0,4},{4,8},{8,12},{12,16},{16,20},{20,24},{24,28},{1,5},{5,9},{9,... | collective-permute-start | bytes 786440 | tf_op jit(solution)/shard_map/while/body/eval_jaxpr/ppermute | solution.py:12
  286.3 11.6 %copy-start.1 = (bf16[256,8,128]{2,0,1:T(8,128)(2,1)}, bf16[256,8,128]{2,0,1:T(8,128)(2,1)S(1)}, u32[]{:S(2)}) copy-start(bf16[256,8,128]{2,0,1:T(8,128)(2,1)S(1)} %convert_element_type.26) | copy-start | bytes 1572868 | tf_op jit(solution)/shard_map/while
  286.9 11.0 %collective-permute-start = (bf16[256,4,128]{2,0,1:T(8,128)(2,1)S(1)}, bf16[256,4,128]{2,0,1:T(8,128)(2,1)S(1)}, u32[]{:S(2)}, u32[]{:S(2)}) collective-permute-start(bf16[256,4,128]{2,0,1:T(8,128)(2,1)S(1)} %bitcast.94), channel_id=1, source_target_pairs={{4,0},{8,4},{12,8},{16,12},{20,16},{24,20},{28,24},{5,1},{9,5},{13... | collective-permute-start | bytes 786440 | tf_op jit(solution)/shard_map/while/body/eval_jaxpr/ppermute | solution.py:12
  288.8 14.8 %collective-permute-start.1 = (bf16[256,4,128]{2,0,1:T(8,128)(2,1)S(1)}, bf16[256,4,128]{2,0,1:T(8,128)(2,1)}, u32[]{:S(2)}, u32[]{:S(2)}) collective-permute-start(bf16[256,4,128]{2,0,1:T(8,128)(2,1)S(1)} %bitcast.95), channel_id=1, source_target_pairs={{0,4},{4,8},{8,12},{12,16},{16,20},{20,24},{24,28},{1,5},{5,9},{9,... | collective-permute-start | bytes 786440 | tf_op jit(solution)/shard_map/while/body/eval_jaxpr/ppermute | solution.py:12
  320.5 11.0 %collective-permute-start = (bf16[256,4,128]{2,0,1:T(8,128)(2,1)S(1)}, bf16[256,4,128]{2,0,1:T(8,128)(2,1)S(1)}, u32[]{:S(2)}, u32[]{:S(2)}) collective-permute-start(bf16[256,4,128]{2,0,1:T(8,128)(2,1)S(1)} %bitcast.94), channel_id=1, source_target_pairs={{4,0},{8,4},{12,8},{16,12},{20,16},{24,20},{28,24},{5,1},{9,5},{13... | collective-permute-start | bytes 786440 | tf_op jit(solution)/shard_map/while/body/eval_jaxpr/ppermute | solution.py:12
  322.4 14.8 %collective-permute-start.1 = (bf16[256,4,128]{2,0,1:T(8,128)(2,1)S(1)}, bf16[256,4,128]{2,0,1:T(8,128)(2,1)}, u32[]{:S(2)}, u32[]{:S(2)}) collective-permute-start(bf16[256,4,128]{2,0,1:T(8,128)(2,1)S(1)} %bitcast.95), channel_id=1, source_target_pairs={{0,4},{4,8},{8,12},{12,16},{16,20},{20,24},{24,28},{1,5},{5,9},{9,... | collective-permute-start | bytes 786440 | tf_op jit(solution)/shard_map/while/body/eval_jaxpr/ppermute | solution.py:12
  354.0 11.0 %collective-permute-start = (bf16[256,4,128]{2,0,1:T(8,128)(2,1)S(1)}, bf16[256,4,128]{2,0,1:T(8,128)(2,1)S(1)}, u32[]{:S(2)}, u32[]{:S(2)}) collective-permute-start(bf16[256,4,128]{2,0,1:T(8,128)(2,1)S(1)} %bitcast.94), channel_id=1, source_target_pairs={{4,0},{8,4},{12,8},{16,12},{20,16},{24,20},{28,24},{5,1},{9,5},{13... | collective-permute-start | bytes 786440 | tf_op jit(solution)/shard_map/while/body/eval_jaxpr/ppermute | solution.py:12
  355.9 14.8 %collective-permute-start.1 = (bf16[256,4,128]{2,0,1:T(8,128)(2,1)S(1)}, bf16[256,4,128]{2,0,1:T(8,128)(2,1)}, u32[]{:S(2)}, u32[]{:S(2)}) collective-permute-start(bf16[256,4,128]{2,0,1:T(8,128)(2,1)S(1)} %bitcast.95), channel_id=1, source_target_pairs={{0,4},{4,8},{8,12},{12,16},{16,20},{20,24},{24,28},{1,5},{5,9},{9,... | collective-permute-start | bytes 786440 | tf_op jit(solution)/shard_map/while/body/eval_jaxpr/ppermute | solution.py:12
  (9 other events, 99.1 us)
Sparse Core Ops, SparseCore 0:
  8.9 37.1 all-gather.1
where the time goes:
time: 396 us; the launch traced here: 395 us
  waiting for transfers between devices  122 us (31%)
  local copies, waits for them, and re-layouts  89 us (22%)
  matrix products  80.4 us (20%)
  starting transfers between devices  68.7 us (17%)
  other arithmetic  19.9 us (5%)
  between operations  14.1 us (4%)
    ppermute x20, waiting for transfers between devices, passed_along(): return lax.ppermute(x, axis, pairs)  83.5 us
    dot_general x10, matrix products, apply_blocks(): jnp.einsum('cbkj,bkij->cbi', picked, blocks, preferred_element_type=jnp.f...  71.6 us
    ppermute x20, starting transfers between devices, passed_along(): return lax.ppermute(x, axis, pairs)  68.7 us
    gather x10, local copies, waits for them, and re-layouts, apply_blocks(): picked = source[:, cols, :]  65.7 us
    all_gather x1, waiting for transfers between devices, body(): lax.all_gather(vectors, 'col', axis=0, tiled=True)  37.4 us
    concatenate x10, other arithmetic, apply_blocks(): source = jnp.concatenate([from_prev, lowered, from_next], axis=1)  11.2 us
    while x36, local copies, waits for them, and re-layouts  9.43 us
    dot_general x1, matrix products, body(): lax.dot_general(rotation, lax.all_gather(vectors, 'col', axis=0, tiled=Tr...  8.72 us
  transfers between devices with their start and end apart: 21, of which 20 were waited for; matrix products, arithmetic and copies ran while one was open for 3% of the time, Pallas kernels for 0%

commit v1 on v0

--- a/solution.py
+++ b/solution.py
@@ -4,6 +4,18 @@
 from jax.sharding import PartitionSpec as P
 
 STEPS = 10
+
+
+def enter_roots_up(my_data, axis_name, which_dim):
+    near, k_now = (lax.axis_size(axis_name), lax.axis_index(axis_name))
+    view_out, earlier = (my_data, 1)
+    while earlier < near:
+        e_now = lax.ppermute(view_out, axis_name, [(jj, jj ^ earlier) for jj in range(near)])
+        found_now = jnp.concatenate([view_out, e_now], axis=which_dim)
+        block_now = jnp.concatenate([e_now, view_out], which_dim)
+        view_out = jnp.where(k_now & earlier == 0, found_now, block_now)
+        earlier = 2 * earlier
+    return view_out
 
 
 def passed_along(x, axis, by):
@@ -29,7 +41,7 @@
     width = blocks.shape[2]
     panel = lax.dot_general(
         rotation,
-        lax.all_gather(vectors, "col", axis=0, tiled=True),
+        enter_roots_up(vectors, "col", 0),
         (((0,), (1,)), ((), ())),
         precision=lax.Precision.HIGHEST,
         preferred_element_type=jnp.float32,

time: 396 us -> 396 us (level)
  between operations: 14.1 us -> 0.77 us
  waiting for transfers between devices: 122 us -> 129 us
    ppermute x0 -> x2, waiting for transfers between devices: none -> 48 us  [enter_roots_up(): lax.ppermute(view_out, axis_name, [(jj, jj ^ earlier) for jj in range(nea...]
    all_gather x1 -> x0, waiting for transfers between devices: 37.4 us -> none  [body(): lax.all_gather(vectors, 'col', axis=0, tiled=True)]
  transfers between devices with their start and end apart: 21 -> 22, of which waited for: 20 -> 21; matrix products, arithmetic and copies ran while one was open for 3% -> 3% of each run, Pallas kernels for 0% -> 0%
where the time goes in v1:
time: 396 us; the launch traced here: 393 us
  waiting for transfers between devices  129 us (33%)
  local copies, waits for them, and re-layouts  90.4 us (23%)
  matrix products  78.3 us (20%)
  starting transfers between devices  72.4 us (18%)
  other arithmetic  21.8 us (6%)
    ppermute x20, waiting for transfers between devices, passed_along(): return lax.ppermute(x, axis, pairs)  80.8 us
    dot_general x10, matrix products, apply_blocks(): jnp.einsum('cbkj,bkij->cbi', picked, blocks, preferred_element_type=jnp.f...  71.6 us
    ppermute x20, starting transfers between devices, passed_along(): return lax.ppermute(x, axis, pairs)  69 us
    gather x10, local copies, waits for them, and re-layouts, apply_blocks(): picked = source[:, cols, :]  65.5 us
    ppermute x2, waiting for transfers between devices, enter_roots_up(): lax.ppermute(view_out, axis_name, [(jj, jj ^ earlier) for jj in range(nea...  48 us
    concatenate x10, other arithmetic, apply_blocks(): source = jnp.concatenate([from_prev, lowered, from_next], axis=1)  11.2 us
    while x36, local copies, waits for them, and re-layouts  9.43 us
  transfers between devices with their start and end apart: 22, of which 21 were waited for; matrix products, arithmetic and copies ran while one was open for 3% of the time, Pallas kernels for 0%

profile of v1, /device:TPU:0, one launch (start us, length us, event | category | flops | bytes accessed | tf_op | source)
XLA Modules:
  0.0 393.4 jit_solution(2413244800748667238)
XLA Ops:
  9.4 45.3 %collective-permute-done.3 = f32[512,1024]{1,0:T(8,128)} collective-permute-done((f32[512,1024]{1,0:T(8,128)S(1)}, f32[512,1024]{1,0:T(8,128)}, u32[]{:S(2)}, u32[]{:S(2)}) %collective-permute-start.3) | collective-permute-done | bytes 2097184 | tf_op jit(solution)/shard_map/ppermute | solution.py:13
  54.8 6.6 %fusion.8 = f32[1024,256]{1,0:T(8,128)} fusion(f32[1024,256]{1,0:T(8,128)S(1)} %copy-done, f32[512,1024]{1,0:T(8,128)} %collective-permute-done.3, f32[512,1024]{1,0:T(8,128)S(1)} %maximum_select_fusion.2, pred[]{:T(512)S(6)} %eq.6), kind=kOutput, calls=%fused_computation.23 | convolution fusion | flops 3224371200 | bytes 6291457 | tf_op jit(solution)/shard_map/dot_general | solution.py:42
  70.4 8.6 %collective-permute-done.4 = bf16[256,4,128]{2,0,1:T(8,128)(2,1)S(1)} collective-permute-done((bf16[256,4,128]{2,0,1:T(8,128)(2,1)S(1)}, bf16[256,4,128]{2,0,1:T(8,128)(2,1)S(1)}, u32[]{:S(2)}, u32[]{:S(2)}) %collective-permute-start.4) | collective-permute-done | bytes 262176 | tf_op jit(solution)/shard_map/ppermute | solution.py:24
  79.1 6.6 %gather_fusion.5 = bf16[128,256,128]{2,1,0:T(8,128)(2,1)} fusion(bf16[256,16,128]{2,0,1:T(8,128)(2,1)S(1)} %pad_maximum_fusion.1, s32[1024]{0:T(1024)S(1)} %pad_clamp_fusion.3), kind=kCustom, calls=%fused_computation.5 | custom fusion | bytes 16777728 | tf_op jit(solution)/shard_map/gather | solution.py:34
  85.7 6.9 %fusion.16 = f32[256,8,128]{2,0,1:T(8,128)S(1)} fusion(bf16[256,8,16,128]{3,0,2,1:T(8,128)(2,1)} %bitcast.90, bf16[8,16,128,128]{3,2,1,0:T(8,128)(2,1)} %param.10, f32[8]{0:T(128)S(1)} %compare_convert_fusion.1), kind=kOutput, calls=%fused_computation.33 | convolution fusion | flops 1074003968 | bytes 13631520 | tf_op jit(solution)/shard_map/cbkj,bkij->cbi/dot_general | solution.py:35
  92.6 299.7 %while.13 = (s32[]{:T(128)}, f32[256,8,128]{2,0,1:T(8,128)}, f32[256,8,128]{2,0,1:T(8,128)S(1)}, s32[1,2,4]{2,1,0:T(2,128)S(1)}, s32[8,16]{1,0:T(8,128)S(1)}, /*...) while((s32[]{:T(128)}, f32[256,8,128]{2,0,1:T(8,128)}, f32[256,8,128]{2,0,1:T(8,128)S(1)}, ...), condition=%wide.region_1.2_spmd.clone, body=%wide.region_0.1_spmd.clone.sunk | while | flops 1075842432 | bytes 44580228 | solution.py:58
  102.1 6.8 %collective-permute-done.1 = bf16[256,4,128]{2,0,1:T(8,128)(2,1)} collective-permute-done((bf16[256,4,128]{2,0,1:T(8,128)(2,1)S(1)}, bf16[256,4,128]{2,0,1:T(8,128)(2,1)}, u32[]{:S(2)}, u32[]{:S(2)}) %collective-permute-start.1) | collective-permute-done | bytes 262176 | tf_op jit(solution)/shard_map/while/body/eval_jaxpr/ppermute | solution.py:24
  110.1 6.6 %gather_fusion.2 = bf16[128,256,128]{2,1,0:T(8,128)(2,1)} fusion(bf16[256,16,128]{2,0,1:T(8,128)(2,1)S(1)} %pad_maximum_fusion.3, s32[1024]{0:T(1024)S(1)} %pad_clamp_fusion.9), kind=kCustom, calls=%fused_computation.2.clone.clone.1 | custom fusion | bytes 16777728 | tf_op jit(solution)/shard_map/while/body/eval_jaxpr/gather | solution.py:34
  116.7 7.2 %fusion.34 = f32[256,8,128]{2,0,1:T(8,128)S(1)} fusion(f32[256,8,128]{2,0,1:T(8,128)} %get-tuple-element.144, bf16[256,8,16,128]{3,0,2,1:T(8,128)(2,1)} %bitcast.89, bf16[8,16,128,128]{3,2,1,0:T(8,128)(2,1)} %get-tuple-element.156, f32[8]{0:T(128)S(1)} %compare_convert_fusion.3), kind=kOutput, calls=%fused_computation.11.clone.1 | convolution fusion | flops 1074528256 | bytes 14680096 | tf_op jit(solution)/shard_map/while/body/eval_jaxpr/cbkj,bkij->cbi/dot_general | solution.py:35
  142.8 6.6 %gather_fusion.2 = bf16[128,256,128]{2,1,0:T(8,128)(2,1)} fusion(bf16[256,16,128]{2,0,1:T(8,128)(2,1)S(1)} %pad_maximum_fusion.3, s32[1024]{0:T(1024)S(1)} %pad_clamp_fusion.9), kind=kCustom, calls=%fused_computation.2.clone.clone.1 | custom fusion | bytes 16777728 | tf_op jit(solution)/shard_map/while/body/eval_jaxpr/gather | solution.py:34
  149.3 7.2 %fusion.34 = f32[256,8,128]{2,0,1:T(8,128)S(1)} fusion(f32[256,8,128]{2,0,1:T(8,128)} %get-tuple-element.144, bf16[256,8,16,128]{3,0,2,1:T(8,128)(2,1)} %bitcast.89, bf16[8,16,128,128]{3,2,1,0:T(8,128)(2,1)} %get-tuple-element.156, f32[8]{0:T(128)S(1)} %compare_convert_fusion.3), kind=kOutput, calls=%fused_computation.11.clone.1 | convolution fusion | flops 1074528256 | bytes 14680096 | tf_op jit(solution)/shard_map/while/body/eval_jaxpr/cbkj,bkij->cbi/dot_general | solution.py:35
  176.3 6.6 %gather_fusion.2 = bf16[128,256,128]{2,1,0:T(8,128)(2,1)} fusion(bf16[256,16,128]{2,0,1:T(8,128)(2,1)S(1)} %pad_maximum_fusion.3, s32[1024]{0:T(1024)S(1)} %pad_clamp_fusion.9), kind=kCustom, calls=%fused_computation.2.clone.clone.1 | custom fusion | bytes 16777728 | tf_op jit(solution)/shard_map/while/body/eval_jaxpr/gather | solution.py:34
  182.9 7.2 %fusion.34 = f32[256,8,128]{2,0,1:T(8,128)S(1)} fusion(f32[256,8,128]{2,0,1:T(8,128)} %get-tuple-element.144, bf16[256,8,16,128]{3,0,2,1:T(8,128)(2,1)} %bitcast.89, bf16[8,16,128,128]{3,2,1,0:T(8,128)(2,1)} %get-tuple-element.156, f32[8]{0:T(128)S(1)} %compare_convert_fusion.3), kind=kOutput, calls=%fused_computation.11.clone.1 | convolution fusion | flops 1074528256 | bytes 14680096 | tf_op jit(solution)/shard_map/while/body/eval_jaxpr/cbkj,bkij->cbi/dot_general | solution.py:35
  209.8 6.6 %gather_fusion.2 = bf16[128,256,128]{2,1,0:T(8,128)(2,1)} fusion(bf16[256,16,128]{2,0,1:T(8,128)(2,1)S(1)} %pad_maximum_fusion.3, s32[1024]{0:T(1024)S(1)} %pad_clamp_fusion.9), kind=kCustom, calls=%fused_computation.2.clone.clone.1 | custom fusion | bytes 16777728 | tf_op jit(solution)/shard_map/while/body/eval_jaxpr/gather | solution.py:34
  216.4 7.2 %fusion.34 = f32[256,8,128]{2,0,1:T(8,128)S(1)} fusion(f32[256,8,128]{2,0,1:T(8,128)} %get-tuple-element.144, bf16[256,8,16,128]{3,0,2,1:T(8,128)(2,1)} %bitcast.89, bf16[8,16,128,128]{3,2,1,0:T(8,128)(2,1)} %get-tuple-element.156, f32[8]{0:T(128)S(1)} %compare_convert_fusion.3), kind=kOutput, calls=%fused_computation.11.clone.1 | convolution fusion | flops 1074528256 | bytes 14680096 | tf_op jit(solution)/shard_map/while/body/eval_jaxpr/cbkj,bkij->cbi/dot_general | solution.py:35
  243.4 6.6 %gather_fusion.2 = bf16[128,256,128]{2,1,0:T(8,128)(2,1)} fusion(bf16[256,16,128]{2,0,1:T(8,128)(2,1)S(1)} %pad_maximum_fusion.3, s32[1024]{0:T(1024)S(1)} %pad_clamp_fusion.9), kind=kCustom, calls=%fused_computation.2.clone.clone.1 | custom fusion | bytes 16777728 | tf_op jit(solution)/shard_map/while/body/eval_jaxpr/gather | solution.py:34
  249.9 7.2 %fusion.34 = f32[256,8,128]{2,0,1:T(8,128)S(1)} fusion(f32[256,8,128]{2,0,1:T(8,128)} %get-tuple-element.144, bf16[256,8,16,128]{3,0,2,1:T(8,128)(2,1)} %bitcast.89, bf16[8,16,128,128]{3,2,1,0:T(8,128)(2,1)} %get-tuple-element.156, f32[8]{0:T(128)S(1)} %compare_convert_fusion.3), kind=kOutput, calls=%fused_computation.11.clone.1 | convolution fusion | flops 1074528256 | bytes 14680096 | tf_op jit(solution)/shard_map/while/body/eval_jaxpr/cbkj,bkij->cbi/dot_general | solution.py:35
  276.9 6.6 %gather_fusion.2 = bf16[128,256,128]{2,1,0:T(8,128)(2,1)} fusion(bf16[256,16,128]{2,0,1:T(8,128)(2,1)S(1)} %pad_maximum_fusion.3, s32[1024]{0:T(1024)S(1)} %pad_clamp_fusion.9), kind=kCustom, calls=%fused_computation.2.clone.clone.1 | custom fusion | bytes 16777728 | tf_op jit(solution)/shard_map/while/body/eval_jaxpr/gather | solution.py:34
  283.5 7.2 %fusion.34 = f32[256,8,128]{2,0,1:T(8,128)S(1)} fusion(f32[256,8,128]{2,0,1:T(8,128)} %get-tuple-element.144, bf16[256,8,16,128]{3,0,2,1:T(8,128)(2,1)} %bitcast.89, bf16[8,16,128,128]{3,2,1,0:T(8,128)(2,1)} %get-tuple-element.156, f32[8]{0:T(128)S(1)} %compare_convert_fusion.3), kind=kOutput, calls=%fused_computation.11.clone.1 | convolution fusion | flops 1074528256 | bytes 14680096 | tf_op jit(solution)/shard_map/while/body/eval_jaxpr/cbkj,bkij->cbi/dot_general | solution.py:35
  310.4 6.6 %gather_fusion.2 = bf16[128,256,128]{2,1,0:T(8,128)(2,1)} fusion(bf16[256,16,128]{2,0,1:T(8,128)(2,1)S(1)} %pad_maximum_fusion.3, s32[1024]{0:T(1024)S(1)} %pad_clamp_fusion.9), kind=kCustom, calls=%fused_computation.2.clone.clone.1 | custom fusion | bytes 16777728 | tf_op jit(solution)/shard_map/while/body/eval_jaxpr/gather | solution.py:34
  317.0 7.2 %fusion.34 = f32[256,8,128]{2,0,1:T(8,128)S(1)} fusion(f32[256,8,128]{2,0,1:T(8,128)} %get-tuple-element.144, bf16[256,8,16,128]{3,0,2,1:T(8,128)(2,1)} %bitcast.89, bf16[8,16,128,128]{3,2,1,0:T(8,128)(2,1)} %get-tuple-element.156, f32[8]{0:T(128)S(1)} %compare_convert_fusion.3), kind=kOutput, calls=%fused_computation.11.clone.1 | convolution fusion | flops 1074528256 | bytes 14680096 | tf_op jit(solution)/shard_map/while/body/eval_jaxpr/cbkj,bkij->cbi/dot_general | solution.py:35
  344.0 6.6 %gather_fusion.2 = bf16[128,256,128]{2,1,0:T(8,128)(2,1)} fusion(bf16[256,16,128]{2,0,1:T(8,128)(2,1)S(1)} %pad_maximum_fusion.3, s32[1024]{0:T(1024)S(1)} %pad_clamp_fusion.9), kind=kCustom, calls=%fused_computation.2.clone.clone.1 | custom fusion | bytes 16777728 | tf_op jit(solution)/shard_map/while/body/eval_jaxpr/gather | solution.py:34
  350.5 7.2 %fusion.34 = f32[256,8,128]{2,0,1:T(8,128)S(1)} fusion(f32[256,8,128]{2,0,1:T(8,128)} %get-tuple-element.144, bf16[256,8,16,128]{3,0,2,1:T(8,128)(2,1)} %bitcast.89, bf16[8,16,128,128]{3,2,1,0:T(8,128)(2,1)} %get-tuple-element.156, f32[8]{0:T(128)S(1)} %compare_convert_fusion.3), kind=kOutput, calls=%fused_computation.11.clone.1 | convolution fusion | flops 1074528256 | bytes 14680096 | tf_op jit(solution)/shard_map/while/body/eval_jaxpr/cbkj,bkij->cbi/dot_general | solution.py:35
  384.1 7.2 %fusion.34 = f32[256,8,128]{2,0,1:T(8,128)S(1)} fusion(f32[256,8,128]{2,0,1:T(8,128)} %get-tuple-element.144, bf16[256,8,16,128]{3,0,2,1:T(8,128)(2,1)} %bitcast.89, bf16[8,16,128,128]{3,2,1,0:T(8,128)(2,1)} %get-tuple-element.156, f32[8]{0:T(128)S(1)} %compare_convert_fusion.3), kind=kOutput, calls=%fused_computation.11.clone.1 | convolution fusion | flops 1074528256 | bytes 14680096 | tf_op jit(solution)/shard_map/while/body/eval_jaxpr/cbkj,bkij->cbi/dot_general | solution.py:35
  (187 shorter events, 193.7 us)
Async XLA Ops:
  0.0 54.8 %copy-start = (f32[1024,256]{1,0:T(8,128)S(1)}, f32[1024,256]{1,0:T(8,128)}, u32[]{:S(2)}) copy-start(f32[1024,256]{1,0:T(8,128)} %param.9) | copy-start | bytes 3145732
  0.0 3.1 collective-permute-start.2
  5.8 49.0 %collective-permute-start.3 = (f32[512,1024]{1,0:T(8,128)S(1)}, f32[512,1024]{1,0:T(8,128)}, u32[]{:S(2)}, u32[]{:S(2)}) collective-permute-start(f32[512,1024]{1,0:T(8,128)S(1)} %maximum_select_fusion.2), channel_id=1, source_target_pairs={{0,2},{1,3},{2,0},{3,1},{4,6},{5,7},{6,4},{7,5},{8,10},{9,11},{10,... | collective-permute-start | bytes 6291464 | tf_op jit(solution)/shard_map/ppermute | solution.py:13
  64.8 14.2 %collective-permute-start.4 = (bf16[256,4,128]{2,0,1:T(8,128)(2,1)S(1)}, bf16[256,4,128]{2,0,1:T(8,128)(2,1)S(1)}, u32[]{:S(2)}, u32[]{:S(2)}) collective-permute-start(bf16[256,4,128]{2,0,1:T(8,128)(2,1)S(1)} %bitcast.94), channel_id=1, source_target_pairs={{0,4},{4,8},{8,12},{12,16},{16,20},{20,24},{24,28},{1,5},{5,9},{9,... | collective-permute-start | bytes 786440 | tf_op jit(solution)/shard_map/ppermute | solution.py:24
  69.0 10.0 %collective-permute-start.5 = (bf16[256,4,128]{2,0,1:T(8,128)(2,1)S(1)}, bf16[256,4,128]{2,0,1:T(8,128)(2,1)S(1)}, u32[]{:S(2)}, u32[]{:S(2)}) collective-permute-start(bf16[256,4,128]{2,0,1:T(8,128)(2,1)S(1)} %bitcast.95), channel_id=1, source_target_pairs={{4,0},{8,4},{12,8},{16,12},{20,16},{24,20},{28,24},{5,1},{9,5},{13... | collective-permute-start | bytes 786440 | tf_op jit(solution)/shard_map/ppermute | solution.py:24
  93.3 8.7 %collective-permute-start = (bf16[256,4,128]{2,0,1:T(8,128)(2,1)S(1)}, bf16[256,4,128]{2,0,1:T(8,128)(2,1)S(1)}, u32[]{:S(2)}, u32[]{:S(2)}) collective-permute-start(bf16[256,4,128]{2,0,1:T(8,128)(2,1)S(1)} %bitcast.91), channel_id=1, source_target_pairs={{4,0},{8,4},{12,8},{16,12},{20,16},{24,20},{28,24},{5,1},{9,5},{13... | collective-permute-start | bytes 786440 | tf_op jit(solution)/shard_map/while/body/eval_jaxpr/ppermute | solution.py:24
  95.2 13.7 %collective-permute-start.1 = (bf16[256,4,128]{2,0,1:T(8,128)(2,1)S(1)}, bf16[256,4,128]{2,0,1:T(8,128)(2,1)}, u32[]{:S(2)}, u32[]{:S(2)}) collective-permute-start(bf16[256,4,128]{2,0,1:T(8,128)(2,1)S(1)} %bitcast.92), channel_id=1, source_target_pairs={{0,4},{4,8},{8,12},{12,16},{16,20},{20,24},{24,28},{1,5},{5,9},{9,... | collective-permute-start | bytes 786440 | tf_op jit(solution)/shard_map/while/body/eval_jaxpr/ppermute | solution.py:24
  125.7 10.1 %collective-permute-start = (bf16[256,4,128]{2,0,1:T(8,128)(2,1)S(1)}, bf16[256,4,128]{2,0,1:T(8,128)(2,1)S(1)}, u32[]{:S(2)}, u32[]{:S(2)}) collective-permute-start(bf16[256,4,128]{2,0,1:T(8,128)(2,1)S(1)} %bitcast.91), channel_id=1, source_target_pairs={{4,0},{8,4},{12,8},{16,12},{20,16},{24,20},{28,24},{5,1},{9,5},{13... | collective-permute-start | bytes 786440 | tf_op jit(solution)/shard_map/while/body/eval_jaxpr/ppermute | solution.py:24
  127.6 14.0 %collective-permute-start.1 = (bf16[256,4,128]{2,0,1:T(8,128)(2,1)S(1)}, bf16[256,4,128]{2,0,1:T(8,128)(2,1)}, u32[]{:S(2)}, u32[]{:S(2)}) collective-permute-start(bf16[256,4,128]{2,0,1:T(8,128)(2,1)S(1)} %bitcast.92), channel_id=1, source_target_pairs={{0,4},{4,8},{8,12},{12,16},{16,20},{20,24},{24,28},{1,5},{5,9},{9,... | collective-permute-start | bytes 786440 | tf_op jit(solution)/shard_map/while/body/eval_jaxpr/ppermute | solution.py:24
  158.3 11.0 %collective-permute-start = (bf16[256,4,128]{2,0,1:T(8,128)(2,1)S(1)}, bf16[256,4,128]{2,0,1:T(8,128)(2,1)S(1)}, u32[]{:S(2)}, u32[]{:S(2)}) collective-permute-start(bf16[256,4,128]{2,0,1:T(8,128)(2,1)S(1)} %bitcast.91), channel_id=1, source_target_pairs={{4,0},{8,4},{12,8},{16,12},{20,16},{24,20},{28,24},{5,1},{9,5},{13... | collective-permute-start | bytes 786440 | tf_op jit(solution)/shard_map/while/body/eval_jaxpr/ppermute | solution.py:24
  160.2 14.8 %collective-permute-start.1 = (bf16[256,4,128]{2,0,1:T(8,128)(2,1)S(1)}, bf16[256,4,128]{2,0,1:T(8,128)(2,1)}, u32[]{:S(2)}, u32[]{:S(2)}) collective-permute-start(bf16[256,4,128]{2,0,1:T(8,128)(2,1)S(1)} %bitcast.92), channel_id=1, source_target_pairs={{0,4},{4,8},{8,12},{12,16},{16,20},{20,24},{24,28},{1,5},{5,9},{9,... | collective-permute-start | bytes 786440 | tf_op jit(solution)/shard_map/while/body/eval_jaxpr/ppermute | solution.py:24
  191.2 11.6 %copy-start.1 = (bf16[256,8,128]{2,0,1:T(8,128)(2,1)}, bf16[256,8,128]{2,0,1:T(8,128)(2,1)S(1)}, u32[]{:S(2)}) copy-start(bf16[256,8,128]{2,0,1:T(8,128)(2,1)S(1)} %convert_element_type.26) | copy-start | bytes 1572868 | tf_op jit(solution)/shard_map/while
  191.9 11.0 %collective-permute-start = (bf16[256,4,128]{2,0,1:T(8,128)(2,1)S(1)}, bf16[256,4,128]{2,0,1:T(8,128)(2,1)S(1)}, u32[]{:S(2)}, u32[]{:S(2)}) collective-permute-start(bf16[256,4,128]{2,0,1:T(8,128)(2,1)S(1)} %bitcast.91), channel_id=1, source_target_pairs={{4,0},{8,4},{12,8},{16,12},{20,16},{24,20},{28,24},{5,1},{9,5},{13... | collective-permute-start | bytes 786440 | tf_op jit(solution)/shard_map/while/body/eval_jaxpr/ppermute | solution.py:24
  193.8 14.8 %collective-permute-start.1 = (bf16[256,4,128]{2,0,1:T(8,128)(2,1)S(1)}, bf16[256,4,128]{2,0,1:T(8,128)(2,1)}, u32[]{:S(2)}, u32[]{:S(2)}) collective-permute-start(bf16[256,4,128]{2,0,1:T(8,128)(2,1)S(1)} %bitcast.92), channel_id=1, source_target_pairs={{0,4},{4,8},{8,12},{12,16},{16,20},{20,24},{24,28},{1,5},{5,9},{9,... | collective-permute-start | bytes 786440 | tf_op jit(solution)/shard_map/while/body/eval_jaxpr/ppermute | solution.py:24
  225.4 11.0 %collective-permute-start = (bf16[256,4,128]{2,0,1:T(8,128)(2,1)S(1)}, bf16[256,4,128]{2,0,1:T(8,128)(2,1)S(1)}, u32[]{:S(2)}, u32[]{:S(2)}) collective-permute-start(bf16[256,4,128]{2,0,1:T(8,128)(2,1)S(1)} %bitcast.91), channel_id=1, source_target_pairs={{4,0},{8,4},{12,8},{16,12},{20,16},{24,20},{28,24},{5,1},{9,5},{13... | collective-permute-start | bytes 786440 | tf_op jit(solution)/shard_map/while/body/eval_jaxpr/ppermute | solution.py:24
  227.3 14.8 %collective-permute-start.1 = (bf16[256,4,128]{2,0,1:T(8,128)(2,1)S(1)}, bf16[256,4,128]{2,0,1:T(8,128)(2,1)}, u32[]{:S(2)}, u32[]{:S(2)}) collective-permute-start(bf16[256,4,128]{2,0,1:T(8,128)(2,1)S(1)} %bitcast.92), channel_id=1, source_target_pairs={{0,4},{4,8},{8,12},{12,16},{16,20},{20,24},{24,28},{1,5},{5,9},{9,... | collective-permute-start | bytes 786440 | tf_op jit(solution)/shard_map/while/body/eval_jaxpr/ppermute | solution.py:24
  258.9 11.0 %collective-permute-start = (bf16[256,4,128]{2,0,1:T(8,128)(2,1)S(1)}, bf16[256,4,128]{2,0,1:T(8,128)(2,1)S(1)}, u32[]{:S(2)}, u32[]{:S(2)}) collective-permute-start(bf16[256,4,128]{2,0,1:T(8,128)(2,1)S(1)} %bitcast.91), channel_id=1, source_target_pairs={{4,0},{8,4},{12,8},{16,12},{20,16},{24,20},{28,24},{5,1},{9,5},{13... | collective-permute-start | bytes 786440 | tf_op jit(solution)/shard_map/while/body/eval_jaxpr/ppermute | solution.py:24
  260.8 14.8 %collective-permute-start.1 = (bf16[256,4,128]{2,0,1:T(8,128)(2,1)S(1)}, bf16[256,4,128]{2,0,1:T(8,128)(2,1)}, u32[]{:S(2)}, u32[]{:S(2)}) collective-permute-start(bf16[256,4,128]{2,0,1:T(8,128)(2,1)S(1)} %bitcast.92), channel_id=1, source_target_pairs={{0,4},{4,8},{8,12},{12,16},{16,20},{20,24},{24,28},{1,5},{5,9},{9,... | collective-permute-start | bytes 786440 | tf_op jit(solution)/shard_map/while/body/eval_jaxpr/ppermute | solution.py:24
  292.5 11.0 %collective-permute-start = (bf16[256,4,128]{2,0,1:T(8,128)(2,1)S(1)}, bf16[256,4,128]{2,0,1:T(8,128)(2,1)S(1)}, u32[]{:S(2)}, u32[]{:S(2)}) collective-permute-start(bf16[256,4,128]{2,0,1:T(8,128)(2,1)S(1)} %bitcast.91), channel_id=1, source_target_pairs={{4,0},{8,4},{12,8},{16,12},{20,16},{24,20},{28,24},{5,1},{9,5},{13... | collective-permute-start | bytes 786440 | tf_op jit(solution)/shard_map/while/body/eval_jaxpr/ppermute | solution.py:24
  294.4 14.8 %collective-permute-start.1 = (bf16[256,4,128]{2,0,1:T(8,128)(2,1)S(1)}, bf16[256,4,128]{2,0,1:T(8,128)(2,1)}, u32[]{:S(2)}, u32[]{:S(2)}) collective-permute-start(bf16[256,4,128]{2,0,1:T(8,128)(2,1)S(1)} %bitcast.92), channel_id=1, source_target_pairs={{0,4},{4,8},{8,12},{12,16},{16,20},{20,24},{24,28},{1,5},{5,9},{9,... | collective-permute-start | bytes 786440 | tf_op jit(solution)/shard_map/while/body/eval_jaxpr/ppermute | solution.py:24
  326.0 11.0 %collective-permute-start = (bf16[256,4,128]{2,0,1:T(8,128)(2,1)S(1)}, bf16[256,4,128]{2,0,1:T(8,128)(2,1)S(1)}, u32[]{:S(2)}, u32[]{:S(2)}) collective-permute-start(bf16[256,4,128]{2,0,1:T(8,128)(2,1)S(1)} %bitcast.91), channel_id=1, source_target_pairs={{4,0},{8,4},{12,8},{16,12},{20,16},{24,20},{28,24},{5,1},{9,5},{13... | collective-permute-start | bytes 786440 | tf_op jit(solution)/shard_map/while/body/eval_jaxpr/ppermute | solution.py:24
  327.9 14.8 %collective-permute-start.1 = (bf16[256,4,128]{2,0,1:T(8,128)(2,1)S(1)}, bf16[256,4,128]{2,0,1:T(8,128)(2,1)}, u32[]{:S(2)}, u32[]{:S(2)}) collective-permute-start(bf16[256,4,128]{2,0,1:T(8,128)(2,1)S(1)} %bitcast.92), channel_id=1, source_target_pairs={{0,4},{4,8},{8,12},{12,16},{16,20},{20,24},{24,28},{1,5},{5,9},{9,... | collective-permute-start | bytes 786440 | tf_op jit(solution)/shard_map/while/body/eval_jaxpr/ppermute | solution.py:24
  359.5 11.0 %collective-permute-start = (bf16[256,4,128]{2,0,1:T(8,128)(2,1)S(1)}, bf16[256,4,128]{2,0,1:T(8,128)(2,1)S(1)}, u32[]{:S(2)}, u32[]{:S(2)}) collective-permute-start(bf16[256,4,128]{2,0,1:T(8,128)(2,1)S(1)} %bitcast.91), channel_id=1, source_target_pairs={{4,0},{8,4},{12,8},{16,12},{20,16},{24,20},{28,24},{5,1},{9,5},{13... | collective-permute-start | bytes 786440 | tf_op jit(solution)/shard_map/while/body/eval_jaxpr/ppermute | solution.py:24
  361.4 14.8 %collective-permute-start.1 = (bf16[256,4,128]{2,0,1:T(8,128)(2,1)S(1)}, bf16[256,4,128]{2,0,1:T(8,128)(2,1)}, u32[]{:S(2)}, u32[]{:S(2)}) collective-permute-start(bf16[256,4,128]{2,0,1:T(8,128)(2,1)S(1)} %bitcast.92), channel_id=1, source_target_pairs={{0,4},{4,8},{8,12},{12,16},{16,20},{20,24},{24,28},{1,5},{5,9},{9,... | collective-permute-start | bytes 786440 | tf_op jit(solution)/shard_map/while/body/eval_jaxpr/ppermute | solution.py:24
  (10 other events, 108.1 us)
